TPU v7x, 32 devices: a whole 2x2x4 slice. The times are simulated.
32 devices in a mesh: ctx: 8 (over z, x), exp: 4 (over y, core).
Axes of the slice: x: 2, y: 2, z: 4, core: 2. Of those that a mesh axis runs over, the one named last changes fastest.
Arguments:
- residual: bfloat16 [4, 1024, 2048], P('exp', 'ctx'), may hold values from -54 to 54
- queries: bfloat16 [4, 1024, 2048], P('exp', 'ctx'), may hold values from -160 to 160
- key_states: bfloat16 [4, 1024, 256], P('exp', 'ctx'), may hold values from -6.1 to 6.1
- value_states: bfloat16 [4, 1024, 256], P('exp', 'ctx'), may hold values from -6 to 6
- expert_ids: int32 [4, 1024, 1], P('exp', 'ctx'), may hold values from 0 to 7; in each aligned block of 128 rows (0 to 127, 128 to 255, ..., all dimensions but the last counted through in order) at most 32 rows name the same one
- route_weight: float32 [4, 1024, 1], P('exp', 'ctx'), may hold values from 0.2 to 1
- gate_weight: bfloat16 [4, 8, 192, 2048], P('exp', 'ctx'), may hold values from -0.125 to 0.125
- up_weight: bfloat16 [4, 8, 192, 2048], P('exp', 'ctx'), may hold values from -0.125 to 0.125
- down_weight: bfloat16 [4, 8, 192, 2048], P('exp', 'ctx'), may hold values from -0.21875 to 0.21875
Outputs:
- output: bfloat16 [4, 1024, 2048], P('exp', 'ctx')
Inputs may be any that keep to these rules, and one draw needn't show every extreme that they name: `expert_ids`: within each aligned block of 128 rows (sequence by sequence, positions in order), which is the rows of one device, no expert is named more than 32 times, a bound that some block reaches; every expert is named somewhere.
All inputs are finite; a program needn't handle non-finite values.
Results may differ from a plain program's by a relative error of at most 0.003.
Values may be sent and summed in bfloat16 or wider, within the bound.
No kernel may reach another device: no remote copies, remote signals or barrier semaphores. Data moves between devices by JAX's collectives and lax.ppermute only.
A program may use at most 64 MiB of HBM per device.

v0:
```python
from functools import partial
import math
import jax
import jax.numpy as jnp
from jax import lax
from jax.sharding import PartitionSpec as P

HD = 128
HEADS = 16
KV_HEADS = 2
PIECES = 4
TOPK = 1
negative_fill = -1e30
epsilon = 1e-06


def contract_rows(left_rows, weight_rows):
    return lax.dot_general(
        left_rows, weight_rows, (((1,), (1,)), ((), ())), preferred_element_type=jnp.float32
    )


def to_groups(half_block, heads_kv, group_size, head_dim):
    token_count = half_block.shape[0]
    shaped = half_block.reshape(token_count, heads_kv, group_size, head_dim)
    return jnp.transpose(shaped, (1, 0, 2, 3)).reshape(heads_kv, token_count * group_size, head_dim)


def keep_current(current):
    return current


def block_update(current, query_rows, query_pos, key_block, value_block, key_start, score_scale):
    running_max, running_total, accumulated = current
    scores = (
        jnp.einsum("gqd,kgd->gqk", query_rows, key_block, preferred_element_type=jnp.float32)
        * score_scale
    )
    key_pos = key_start + jnp.arange(key_block.shape[0], dtype=jnp.int32)
    allowed = key_pos[None, None, :] <= query_pos[None, :, None]
    scores = jnp.where(allowed, scores, negative_fill)
    new_max = jnp.maximum(running_max, jnp.max(scores, axis=-1))
    rescale = jnp.exp(running_max - new_max)
    exponent = jnp.where(allowed, jnp.exp(scores - new_max[..., None]), 0.0)
    new_total = running_total * rescale + jnp.sum(exponent, axis=-1)
    product = jnp.einsum(
        "gqk,kgd->gqd",
        exponent.astype(jnp.bfloat16),
        value_block,
        preferred_element_type=jnp.float32,
    )
    return (new_max, new_total, accumulated * rescale[..., None] + product)


def make_folder(query_sets, position_sets, last_positions, heads_kv, head_dim, score_scale):

    def fold_keys(running, key_piece, first_key):
        key_part, value_part = key_piece
        key_count = key_part.shape[1]
        key_width = math.gcd(key_count, 512)
        key_rows = key_part.reshape(key_count, heads_kv, head_dim)
        value_rows = value_part.reshape(key_count, heads_kv, head_dim)

        def one_block(block_index, current_sets):
            offset = block_index * key_width
            key_block = lax.dynamic_slice_in_dim(key_rows, offset, key_width, 0)
            value_block = lax.dynamic_slice_in_dim(value_rows, offset, key_width, 0)
            updated = []
            for current, query_rows, query_pos, last_pos in zip(
                current_sets, query_sets, position_sets, last_positions
            ):
                step_fn = partial(
                    block_update,
                    query_rows=query_rows,
                    query_pos=query_pos,
                    key_block=key_block,
                    value_block=value_block,
                    key_start=offset,
                    score_scale=score_scale,
                )
                updated.append(lax.cond(offset <= last_pos, step_fn, keep_current, current))
            return tuple(updated)

        return lax.fori_loop(0, key_count // key_width, one_block, running)

    return fold_keys


def finish(current, token_count, heads_kv, group_size, head_dim):
    running_max, running_total, accumulated = current
    result = accumulated / running_total[..., None]
    shaped = result.reshape(heads_kv, token_count, group_size, head_dim)
    return (
        jnp.transpose(shaped, (1, 0, 2, 3))
        .reshape(token_count, heads_kv * group_size * head_dim)
        .astype(jnp.bfloat16)
    )


def shards(
    residual,
    queries,
    key_states,
    value_states,
    expert_ids,
    route_weight,
    gate_weight,
    up_weight,
    down_weight,
):
    ctx_count = lax.axis_size("ctx")
    exp_count = lax.axis_size("exp")
    ctx_rank = lax.axis_index("ctx")
    tok_rows = residual.shape[1]
    half_rows = tok_rows // 2
    group_size = HEADS // KV_HEADS
    score_scale = 1.0 / math.sqrt(HD)
    local_queries = queries[0]
    first_half = local_queries[:half_rows]
    second_half = local_queries[half_rows:]
    first_start = ctx_rank * tok_rows
    second_start = first_start + half_rows
    offsets = jnp.repeat(jnp.arange(half_rows, dtype=jnp.int32), group_size)
    query_sets = (
        to_groups(first_half, KV_HEADS, group_size, HD),
        to_groups(second_half, KV_HEADS, group_size, HD),
    )
    position_sets = (first_start + offsets, second_start + offsets)
    last_positions = (first_start + half_rows - 1, second_start + half_rows - 1)
    row_total = half_rows * group_size
    empty_state = (
        jnp.full((KV_HEADS, row_total), negative_fill, jnp.float32),
        jnp.zeros((KV_HEADS, row_total), jnp.float32),
        jnp.zeros((KV_HEADS, row_total, HD), jnp.float32),
    )
    folder = make_folder(query_sets, position_sets, last_positions, KV_HEADS, HD, score_scale)
    final_sets = folder(
        (empty_state, empty_state),
        (
            lax.all_gather(key_states, "ctx", axis=1, tiled=True),
            lax.all_gather(value_states, "ctx", axis=1, tiled=True),
        ),
        jnp.int32(0),
    )
    first_out = finish(final_sets[0], half_rows, KV_HEADS, group_size, HD)
    second_out = finish(final_sets[1], half_rows, KV_HEADS, group_size, HD)
    attention = jnp.concatenate([first_out, second_out], axis=0)
    summed = residual[0].astype(jnp.float32) + lax.optimization_barrier(attention).astype(
        jnp.float32
    )
    normed = (
        summed * lax.rsqrt(jnp.mean(summed * summed, axis=-1, keepdims=True) + epsilon)
    ).astype(jnp.bfloat16)
    width_model = normed.shape[1]
    experts_each = ctx_count // PIECES
    expert_total = experts_each * exp_count
    pair_count = tok_rows * TOPK
    capacity = max(2, 2 * tok_rows * TOPK // expert_total)
    flat_ids = expert_ids[0].reshape(pair_count)
    onehot = (flat_ids[:, None] == jnp.arange(expert_total, dtype=jnp.int32)[None, :]).astype(
        jnp.int32
    )
    earlier = jnp.cumsum(onehot, axis=0) - onehot
    slot_index = jnp.sum(earlier * onehot, axis=1)
    owner_index = flat_ids // experts_each
    local_expert = flat_ids % experts_each
    target = (local_expert * exp_count + owner_index) * capacity + slot_index
    pair_token = jnp.arange(pair_count, dtype=jnp.int32) // TOPK
    slot_total = expert_total * capacity
    slot_table = jnp.full((slot_total,), tok_rows, jnp.int32).at[target].set(pair_token)
    padded = jnp.concatenate([normed, jnp.zeros((1, width_model), jnp.bfloat16)], axis=0)
    outgoing = padded[slot_table].reshape(experts_each, exp_count, capacity, width_model)
    arrived = lax.all_to_all(outgoing, "exp", split_axis=1, concat_axis=1, tiled=True)
    copies = jnp.broadcast_to(
        arrived[:, None], (experts_each, PIECES, exp_count, capacity, width_model)
    ).reshape(ctx_count, exp_count * capacity, width_model)
    gate_piece = gate_weight[0, 0]
    up_piece = up_weight[0, 0]
    down_piece = down_weight[0, 0]
    received = lax.all_to_all(copies, "ctx", split_axis=0, concat_axis=0, tiled=True)
    sources = received.shape[0]
    item_count = received.shape[1]
    flat_rows = received.reshape(sources * item_count, width_model)
    gate_part = contract_rows(flat_rows, gate_piece)
    up_part = contract_rows(flat_rows, up_piece)
    active = (jax.nn.silu(gate_part) * up_part).astype(jnp.bfloat16)
    partial_out = jnp.dot(active, down_piece, preferred_element_type=jnp.float32).astype(
        jnp.bfloat16
    )
    returned = lax.all_to_all(
        partial_out.reshape(sources, item_count, width_model),
        "ctx",
        split_axis=0,
        concat_axis=0,
        tiled=True,
    )
    piece_sum = jnp.sum(
        returned.reshape(experts_each, PIECES, exp_count, capacity, width_model).astype(
            jnp.float32
        ),
        axis=1,
    ).astype(jnp.bfloat16)
    arrived_back = lax.all_to_all(piece_sum, "exp", split_axis=1, concat_axis=1, tiled=True)
    gathered = arrived_back.reshape(slot_total, width_model)[target].astype(jnp.float32)
    weighted = gathered * route_weight[0]
    mixture = jnp.sum(weighted.reshape(tok_rows, TOPK, width_model), axis=1)
    return (summed + mixture).astype(jnp.bfloat16)[None]


def solution(mesh):
    in_specs = (
        P("exp", "ctx", None),
        P("exp", "ctx", None),
        P("exp", "ctx", None),
        P("exp", "ctx", None),
        P("exp", "ctx", None),
        P("exp", "ctx", None),
        P("exp", "ctx", None, None),
        P("exp", "ctx", None, None),
        P("exp", "ctx", None, None),
    )
    out_specs = P("exp", "ctx", None)
    return jax.shard_map(shards, mesh=mesh, in_specs=in_specs, out_specs=out_specs, check_vma=False)
```

profile of v0, /device:TPU:0, one launch (start us, length us, event | category | flops | bytes accessed | tf_op | source)
XLA Modules:
  0.0 328.2 jit_solution(8292580245410848761)
XLA Ops:
  0.0 1.1 slice_bitcast_fusion
  1.4 29.6 %all_gather.6 = bf16[1,1024,256]{1,2,0:T(8,128)(2,1)S(1)} all-gather(bf16[1,128,256]{1,2,0:T(8,128)(2,1)S(1)} %copy.41), channel_id=1, replica_groups=mesh['ctx'=8,'exp'=4] {'ctx'}, dimensions={1}, use_global_device_ids=true | all-gather | bytes 589824 | tf_op jit(solution)/shard_map/all_gather | solution.py:140
  31.1 27.8 %all_gather.7 = bf16[1,1024,256]{1,2,0:T(8,128)(2,1)S(1)} all-gather(bf16[1,128,256]{1,2,0:T(8,128)(2,1)S(1)} %copy.42), channel_id=1, replica_groups=mesh['ctx'=8,'exp'=4] {'ctx'}, dimensions={1}, use_global_device_ids=true | all-gather | bytes 589824 | tf_op jit(solution)/shard_map/all_gather | solution.py:141
  60.6 9.5 %while.24 = (s32[]{:T(128)}, f32[2,512]{1,0:T(2,128)S(1)}, f32[2,512]{1,0:T(2,128)S(1)}, f32[2,512,128]{2,1,0:T(8,128)}, f32[2,512]{1,0:T(2,128)S(1)}, /*index=5...) while((s32[]{:T(128)}, f32[2,512]{1,0:T(2,128)S(1)}, ...), condition=%wide.region_9.10_spmd.clone, body=%wide.region_0.9_spmd.clone.sunk | while | flops 551557120 | bytes 29000316 | solution.py:84
  61.1 3.4 %conditional.7 = ((f32[2,512]{1,0:T(2,128)S(1)}, f32[2,512]{1,0:T(2,128)S(1)}, f32[2,512,128]{2,1,0:T(8,128)})) conditional(s32[]{:T(128)} %convert_element_type.131, (f32[2,512]{1,0:T(2,128)S(1)}, f32[2,512]{1,0:T(2,128)S(1)}, f32[2,512,128]{2,1,0:T(8,128)}) %tuple.67, (s32[]{:T(128)}, s32[]{:T(128)}, bf16[2,512,128]{2,1,0:T(8,128)(2,1)S(1)}, ...), branch_computations={%region_5.5_spmd, %region_6.8_spmd} | conditional | flops 275778560 | bytes 13449312 | solution.py:81
  62.6 1.1 convolution_add_fusion.1
  64.5 2.6 conditional.6
  66.0 1.1 convolution_add_fusion
  68.4 1.0 copy-done.3
  70.2 1.3 fusion.39
  73.5 1.0 scatter_custom_fusion
  74.5 1.4 gather_fusion
  76.0 17.1 %all_to_all.20 = bf16[2,4,32,2048]{3,2,0,1:T(8,128)(2,1)S(1)} all-to-all(bf16[2,4,32,2048]{3,2,0,1:T(8,128)(2,1)S(1)} %copy.49), channel_id=1, replica_groups=mesh['ctx'=8,'exp'=4] {'exp'}, dimensions={1} | all-to-all | bytes 2097152 | tf_op jit(solution)/shard_map/all_to_all | solution.py:173
  93.7 99.7 %all_to_all.21 = bf16[8,128,2048]{2,1,0:T(8,128)(2,1)S(1)} all-to-all(bf16[8,128,2048]{2,1,0:T(8,128)(2,1)S(1)} %bitcast.91), channel_id=1, replica_groups=mesh['ctx'=8,'exp'=4] {'ctx'}, dimensions={0} | all-to-all | bytes 8388608 | tf_op jit(solution)/shard_map/all_to_all | solution.py:180
  193.4 2.0 copy-done.2
  195.4 2.5 fusion.30
  197.9 7.1 %convolution_convert_fusion = bf16[1024,2048]{1,0:T(8,128)(2,1)} fusion(bf16[1024,2048]{1,0:T(8,128)(2,1)} %bitcast.97, bf16[1,1,192,2048]{3,2,1,0:T(8,128)(2,1)S(1)} %copy-done, bf16[1,1,192,2048]{3,2,1,0:T(8,128)(2,1)S(1)} %copy-done.13, f32[1024,192]{0,1:T(8,128)} %fusion.30), kind=kOutput, calls=%fused_computation.43 | convolution fusion | flops 1613889536 | bytes 10747904 | tf_op jit(solution)/shard_map/dot_general | solution.py:187
  205.0 97.0 %all_to_all.22 = bf16[8,128,2048]{2,1,0:T(8,128)(2,1)} all-to-all(bf16[8,128,2048]{2,1,0:T(8,128)(2,1)} %bitcast.98), channel_id=1, replica_groups=mesh['ctx'=8,'exp'=4] {'ctx'}, dimensions={0} | all-to-all | bytes 8388608 | tf_op jit(solution)/shard_map/all_to_all | solution.py:190
  302.0 3.1 reduce_sum.57
  305.0 1.1 copy.51
  306.1 4.2 %all-to-all-start.3 = ((bf16[2,4,32,2048]{3,2,0,1:T(8,128)(2,1)}), bf16[2,4,32,2048]{3,2,0,1:T(8,128)(2,1)}, u32[]{:S(2)}, u32[]{:S(2)}) async-start(bf16[2,4,32,2048]{3,2,0,1:T(8,128)(2,1)} %copy.51), calls=%async_computation.3 | async-start | bytes 2097152 | tf_op jit(solution)/shard_map/all_to_all | solution.py:203
  310.4 14.5 %all-to-all-done.3 = bf16[2,4,32,2048]{3,2,0,1:T(8,128)(2,1)} async-done(((bf16[2,4,32,2048]{3,2,0,1:T(8,128)(2,1)}), bf16[2,4,32,2048]{3,2,0,1:T(8,128)(2,1)}, u32[]{:S(2)}, u32[]{:S(2)}) %all-to-all-start.3) | async-done | bytes 1048608 | tf_op jit(solution)/shard_map/all_to_all | solution.py:203
  324.9 1.3 copy.52
  327.1 1.1 fusion.37
  (93 shorter events, 11.7 us)
Async XLA Ops:
  0.0 197.9 %copy-start = (bf16[1,1,192,2048]{3,2,1,0:T(8,128)(2,1)S(1)}, bf16[1,1,192,2048]{3,2,1,0:T(8,128)(2,1)}, u32[]{:S(2)}) copy-start(bf16[1,1,192,2048]{3,2,1,0:T(8,128)(2,1)} %param.23) | copy-start | bytes 2359300
  0.0 1.3 copy-start.8
  0.0 30.9 %copy-start.9 = (bf16[1,128,256]{2,1,0:T(8,128)(2,1)S(1)}, bf16[1,128,256]{2,1,0:T(8,128)(2,1)}, u32[]{:S(2)}) copy-start(bf16[1,128,256]{2,1,0:T(8,128)(2,1)} %param.18) | copy-start | bytes 196612
  61.1 3.4 %copy-start.3 = (f32[2,512,128]{2,1,0:T(8,128)S(1)}, f32[2,512,128]{2,1,0:T(8,128)}, u32[]{:S(2)}) copy-start(f32[2,512,128]{2,1,0:T(8,128)} %get-tuple-element.613) | copy-start | bytes 1572868 | tf_op jit(solution)/shard_map/while
  61.5 1.2 copy-start.5
  63.7 0.8 copy-start.6
  67.1 0.8 copy-start.4
  68.3 1.0 copy-start.3
  69.4 0.8 copy-start.4
  70.2 1.5 copy-start.7
  71.5 1.0 copy-start.1
  71.9 1.1 copy-start.10
  93.7 101.7 %copy-start.12 = (bf16[1,1,192,2048]{3,2,1,0:T(8,128)(2,1)S(1)}, bf16[1,1,192,2048]{3,2,1,0:T(8,128)(2,1)}, u32[]{:S(2)}) copy-start(bf16[1,1,192,2048]{3,2,1,0:T(8,128)(2,1)} %param.21) | copy-start | bytes 2359300
  193.4 2.0 copy-start.2
  195.4 2.5 copy-start.13
  306.1 18.8 %all-to-all-start.3 = ((bf16[2,4,32,2048]{3,2,0,1:T(8,128)(2,1)}), bf16[2,4,32,2048]{3,2,0,1:T(8,128)(2,1)}, u32[]{:S(2)}, u32[]{:S(2)}) async-start(bf16[2,4,32,2048]{3,2,0,1:T(8,128)(2,1)} %copy.51), calls=%async_computation.3 | async-start | bytes 2097152 | tf_op jit(solution)/shard_map/all_to_all | solution.py:203
  326.2 1.0 copy-start.11
where the time goes:
time: 329 us; the launch traced here: 328 us
  blocking collectives  271 us (82%)
  local copies, waits for them, and re-layouts  16.7 us (5%)
  waiting for transfers between devices  14.5 us (4%)
  matrix products  12.8 us (4%)
  other arithmetic  8.21 us (2%)
  starting transfers between devices  4.23 us (1%)
    all_to_all x1, blocking collectives, shards(): lax.all_to_all(copies, 'ctx', split_axis=0, concat_axis=0, tiled=True)  99.7 us
    all_to_all x1, blocking collectives, shards(): lax.all_to_all(partial_out.reshape(sources, item_count, width_model), 'ct...  97 us
    all_gather x1, blocking collectives, shards(): lax.all_gather(key_states, 'ctx', axis=1, tiled=True)  29.6 us
    all_gather x1, blocking collectives, shards(): lax.all_gather(value_states, 'ctx', axis=1, tiled=True)  27.8 us
    all_to_all x1, blocking collectives, shards(): lax.all_to_all(outgoing, 'exp', split_axis=1, concat_axis=1, tiled=True)  17.1 us
    all_to_all x1, waiting for transfers between devices, shards(): lax.all_to_all(piece_sum, 'exp', split_axis=1, concat_axis=1, tiled=True)  14.5 us
    dot_general x1, matrix products, shards(): jnp.dot(active, down_piece, preferred_element_type=jnp.float32)  7.06 us
  transfers between devices with their start and end apart: 1, of which 1 were waited for; matrix products, arithmetic and copies ran while one was open for 0% of the time, Pallas kernels for 0%

commit v1 on v0

--- a/solution.py
+++ b/solution.py
@@ -12,6 +12,17 @@
 TOPK = 1
 negative_fill = -1e30
 epsilon = 1e-06
+
+
+def in_blocks(value, dim, length):
+    before, after = (value.shape[:dim], value.shape[dim + 1 :])
+    return jnp.moveaxis(value.reshape(*before, length, -1, *after), dim, 0)
+
+
+def in_order(blocks, dim):
+    blocks = jnp.moveaxis(blocks, 0, dim)
+    lengths = blocks.shape
+    return blocks.reshape(*lengths[:dim], lengths[dim] * lengths[dim + 1], *lengths[dim + 2 :])
 
 
 def contract_rows(left_rows, weight_rows):
@@ -170,7 +181,14 @@
     slot_table = jnp.full((slot_total,), tok_rows, jnp.int32).at[target].set(pair_token)
     padded = jnp.concatenate([normed, jnp.zeros((1, width_model), jnp.bfloat16)], axis=0)
     outgoing = padded[slot_table].reshape(experts_each, exp_count, capacity, width_model)
-    arrived = lax.all_to_all(outgoing, "exp", split_axis=1, concat_axis=1, tiled=True)
+    size, index = (lax.axis_size("exp"), lax.axis_index("exp"))
+    tiles = in_blocks(outgoing, 1, size)
+    gathered_2 = [tiles[index]]
+    for step in range(1, size):
+        sent = tiles[index ^ step]
+        gathered_2.append(lax.ppermute(sent, "exp", [(i, i ^ step) for i in range(size)]))
+    tiles = jnp.stack(gathered_2)[index ^ jnp.arange(size)]
+    arrived = in_order(tiles, 1)
     copies = jnp.broadcast_to(
         arrived[:, None], (experts_each, PIECES, exp_count, capacity, width_model)
     ).reshape(ctx_count, exp_count * capacity, width_model)

time: 329 us -> 329 us (level)
  blocking collectives: 271 us -> 255 us
  waiting for transfers between devices: 14.5 us -> 26.5 us
    all_to_all x1 -> x0, blocking collectives: 17.1 us -> none  [shards(): lax.all_to_all(outgoing, 'exp', split_axis=1, concat_axis=1, tiled=True)]
    ppermute x0 -> x3, waiting for transfers between devices: none -> 12 us  [shards(): lax.ppermute(sent, 'exp', [(i, i ^ step) for i in range(size)])]
  transfers between devices with their start and end apart: 1 -> 4, of which waited for: 1 -> 3; matrix products, arithmetic and copies ran while one was open for 0% -> 0% of each run, Pallas kernels for 0% -> 0%
where the time goes in v1:
time: 329 us
  blocking collectives  255 us (78%)
  waiting for transfers between devices  26.5 us (8%)
  local copies, waits for them, and re-layouts  19.5 us (6%)
  matrix products  12.8 us (4%)
  other arithmetic  8.35 us (3%)
  starting transfers between devices  6.17 us (2%)
    all_to_all x1, blocking collectives, shards(): lax.all_to_all(copies, 'ctx', split_axis=0, concat_axis=0, tiled=True)  100 us
    all_to_all x1, blocking collectives, shards(): lax.all_to_all(partial_out.reshape(sources, item_count, width_model), 'ct...  97.2 us
    all_gather x1, blocking collectives, shards(): lax.all_gather(key_states, 'ctx', axis=1, tiled=True)  29.6 us
    all_gather x1, blocking collectives, shards(): lax.all_gather(value_states, 'ctx', axis=1, tiled=True)  27.8 us
    all_to_all x1, waiting for transfers between devices, shards(): lax.all_to_all(piece_sum, 'exp', split_axis=1, concat_axis=1, tiled=True)  14.5 us
    ppermute x3, waiting for transfers between devices, shards(): lax.ppermute(sent, 'exp', [(i, i ^ step) for i in range(size)])  12 us
    dot_general x1, matrix products, shards(): jnp.dot(active, down_piece, preferred_element_type=jnp.float32)  7.06 us
  transfers between devices with their start and end apart: 4, of which 3 were waited for; matrix products, arithmetic and copies ran while one was open for 0% of the time, Pallas kernels for 0%

profile of v1, /device:TPU:0, one launch (start us, length us, event | category | flops | bytes accessed | tf_op | source)
XLA Modules:
  0.0 328.9 jit_solution(16171580885751667377)
XLA Ops:
  0.0 1.2 slice_bitcast_fusion
  1.4 29.6 %all_gather.6 = bf16[1,1024,256]{1,2,0:T(8,128)(2,1)S(1)} all-gather(bf16[1,128,256]{1,2,0:T(8,128)(2,1)S(1)} %copy.51), channel_id=1, replica_groups=mesh['ctx'=8,'exp'=4] {'ctx'}, dimensions={1}, use_global_device_ids=true | all-gather | bytes 589824 | tf_op jit(solution)/shard_map/all_gather | solution.py:151
  31.1 27.8 %all_gather.7 = bf16[1,1024,256]{1,2,0:T(8,128)(2,1)S(1)} all-gather(bf16[1,128,256]{1,2,0:T(8,128)(2,1)S(1)} %copy.52), channel_id=1, replica_groups=mesh['ctx'=8,'exp'=4] {'ctx'}, dimensions={1}, use_global_device_ids=true | all-gather | bytes 589824 | tf_op jit(solution)/shard_map/all_gather | solution.py:152
  60.7 9.5 %while.24 = (s32[]{:T(128)}, f32[2,512]{1,0:T(2,128)S(1)}, f32[2,512]{1,0:T(2,128)S(1)}, f32[2,512,128]{2,1,0:T(8,128)}, f32[2,512]{1,0:T(2,128)S(1)}, /*index=5...) while((s32[]{:T(128)}, f32[2,512]{1,0:T(2,128)S(1)}, ...), condition=%wide.region_9.10_spmd.clone, body=%wide.region_0.9_spmd.clone.sunk | while | flops 551557120 | bytes 29000316 | solution.py:95
  61.1 3.4 %conditional.7 = ((f32[2,512]{1,0:T(2,128)S(1)}, f32[2,512]{1,0:T(2,128)S(1)}, f32[2,512,128]{2,1,0:T(8,128)})) conditional(s32[]{:T(128)} %convert_element_type.131, (f32[2,512]{1,0:T(2,128)S(1)}, f32[2,512]{1,0:T(2,128)S(1)}, f32[2,512,128]{2,1,0:T(8,128)}) %tuple.71, (s32[]{:T(128)}, s32[]{:T(128)}, bf16[2,512,128]{2,1,0:T(8,128)(2,1)S(1)}, ...), branch_computations={%region_5.5_spmd, %region_6.8_spmd} | conditional | flops 275778560 | bytes 13449312 | solution.py:92
  62.7 1.1 convolution_add_fusion.1
  64.6 2.6 conditional.6
  70.2 1.3 fusion.39
  74.6 1.4 gather_fusion
  76.1 1.6 collective-permute-start.1
  78.0 7.3 %collective-permute-done.1 = bf16[2,1,32,2048]{3,2,0,1:T(8,128)(2,1)S(1)} collective-permute-done((bf16[2,1,32,2048]{3,2,0,1:T(8,128)(2,1)S(1)}, bf16[2,1,32,2048]{3,2,0,1:T(8,128)(2,1)S(1)}, u32[]{:S(2)}, u32[]{:S(2)}) %collective-permute-start.1) | collective-permute-done | bytes 262176 | tf_op jit(solution)/shard_map/ppermute | solution.py:189
  85.3 4.7 %collective-permute-done.2 = bf16[2,1,32,2048]{3,2,0,1:T(8,128)(2,1)S(1)} collective-permute-done((bf16[2,1,32,2048]{3,2,0,1:T(8,128)(2,1)S(1)}, bf16[2,1,32,2048]{3,2,0,1:T(8,128)(2,1)S(1)}, u32[]{:S(2)}, u32[]{:S(2)}) %collective-permute-start.2) | collective-permute-done | bytes 262176 | tf_op jit(solution)/shard_map/ppermute | solution.py:189
  90.1 1.6 gather_fusion.1
  91.7 1.3 copy_bitcast_fusion
  93.6 100.3 %all_to_all.15 = bf16[8,128,2048]{2,1,0:T(8,128)(2,1)S(1)} all-to-all(bf16[8,128,2048]{2,1,0:T(8,128)(2,1)S(1)} %bitcast.113), channel_id=1, replica_groups=mesh['ctx'=8,'exp'=4] {'ctx'}, dimensions={0} | all-to-all | bytes 8388608 | tf_op jit(solution)/shard_map/all_to_all | solution.py:198
  193.9 2.0 copy-done.2
  195.9 2.5 fusion.30
  198.4 7.1 %convolution_convert_fusion = bf16[1024,2048]{1,0:T(8,128)(2,1)} fusion(bf16[1024,2048]{1,0:T(8,128)(2,1)} %bitcast.119, bf16[1,1,192,2048]{3,2,1,0:T(8,128)(2,1)S(1)} %copy-done, bf16[1,1,192,2048]{3,2,1,0:T(8,128)(2,1)S(1)} %copy-done.13, f32[1024,192]{0,1:T(8,128)} %fusion.30), kind=kOutput, calls=%fused_computation.44 | convolution fusion | flops 1613889536 | bytes 10747904 | tf_op jit(solution)/shard_map/dot_general | solution.py:205
  205.4 97.2 %all_to_all.16 = bf16[8,128,2048]{2,1,0:T(8,128)(2,1)} all-to-all(bf16[8,128,2048]{2,1,0:T(8,128)(2,1)} %bitcast.120), channel_id=1, replica_groups=mesh['ctx'=8,'exp'=4] {'ctx'}, dimensions={0} | all-to-all | bytes 8388608 | tf_op jit(solution)/shard_map/all_to_all | solution.py:208
  302.6 3.1 reduce_sum.57
  305.7 1.1 copy.60
  306.8 4.2 %all-to-all-start.2 = ((bf16[2,4,32,2048]{3,2,0,1:T(8,128)(2,1)}), bf16[2,4,32,2048]{3,2,0,1:T(8,128)(2,1)}, u32[]{:S(2)}, u32[]{:S(2)}) async-start(bf16[2,4,32,2048]{3,2,0,1:T(8,128)(2,1)} %copy.60), calls=%async_computation.2 | async-start | bytes 2097152 | tf_op jit(solution)/shard_map/all_to_all | solution.py:221
  311.0 14.5 %all-to-all-done.2 = bf16[2,4,32,2048]{3,2,0,1:T(8,128)(2,1)} async-done(((bf16[2,4,32,2048]{3,2,0,1:T(8,128)(2,1)}), bf16[2,4,32,2048]{3,2,0,1:T(8,128)(2,1)}, u32[]{:S(2)}, u32[]{:S(2)}) %all-to-all-start.2) | async-done | bytes 1048608 | tf_op jit(solution)/shard_map/all_to_all | solution.py:221
  325.6 1.3 copy.61
  (102 shorter events, 16.3 us)
Async XLA Ops:
  0.0 198.4 %copy-start = (bf16[1,1,192,2048]{3,2,1,0:T(8,128)(2,1)S(1)}, bf16[1,1,192,2048]{3,2,1,0:T(8,128)(2,1)}, u32[]{:S(2)}) copy-start(bf16[1,1,192,2048]{3,2,1,0:T(8,128)(2,1)} %param.23) | copy-start | bytes 2359300
  0.0 1.3 copy-start.8
  0.0 31.0 %copy-start.9 = (bf16[1,128,256]{2,1,0:T(8,128)(2,1)S(1)}, bf16[1,128,256]{2,1,0:T(8,128)(2,1)}, u32[]{:S(2)}) copy-start(bf16[1,128,256]{2,1,0:T(8,128)(2,1)} %param.18) | copy-start | bytes 196612
  61.1 3.4 %copy-start.3 = (f32[2,512,128]{2,1,0:T(8,128)S(1)}, f32[2,512,128]{2,1,0:T(8,128)}, u32[]{:S(2)}) copy-start(f32[2,512,128]{2,1,0:T(8,128)} %get-tuple-element.632) | copy-start | bytes 1572868 | tf_op jit(solution)/shard_map/while
  61.5 1.2 copy-start.5
  63.7 0.8 copy-start.6
  67.2 0.8 copy-start.4
  68.4 1.0 copy-start.3
  69.4 0.8 copy-start.4
  70.2 1.5 copy-start.7
  71.5 1.0 copy-start.1
  71.9 1.1 copy-start.10
  76.0 2.0 collective-permute-start
  76.1 9.2 %collective-permute-start.1 = (bf16[2,1,32,2048]{3,2,0,1:T(8,128)(2,1)S(1)}, bf16[2,1,32,2048]{3,2,0,1:T(8,128)(2,1)S(1)}, u32[]{:S(2)}, u32[]{:S(2)}) collective-permute-start(bf16[2,1,32,2048]{3,2,0,1:T(8,128)(2,1)S(1)} %get-tuple-element.485), channel_id=1, source_target_pairs={{0,2},{1,3},{2,0},{3,1},{4,6},{5,7},{6,4},{7,5},{8,10},{9,11},{10,... | collective-permute-start | bytes 786440 | tf_op jit(solution)/shard_map/ppermute | solution.py:189
  77.7 12.3 %collective-permute-start.2 = (bf16[2,1,32,2048]{3,2,0,1:T(8,128)(2,1)S(1)}, bf16[2,1,32,2048]{3,2,0,1:T(8,128)(2,1)S(1)}, u32[]{:S(2)}, u32[]{:S(2)}) collective-permute-start(bf16[2,1,32,2048]{3,2,0,1:T(8,128)(2,1)S(1)} %get-tuple-element.484), channel_id=1, source_target_pairs={{0,3},{1,2},{2,1},{3,0},{4,7},{5,6},{6,5},{7,4},{8,11},{9,10},{10,... | collective-permute-start | bytes 786440 | tf_op jit(solution)/shard_map/ppermute | solution.py:189
  93.6 102.3 %copy-start.12 = (bf16[1,1,192,2048]{3,2,1,0:T(8,128)(2,1)S(1)}, bf16[1,1,192,2048]{3,2,1,0:T(8,128)(2,1)}, u32[]{:S(2)}) copy-start(bf16[1,1,192,2048]{3,2,1,0:T(8,128)(2,1)} %param.21) | copy-start | bytes 2359300
  193.9 2.0 copy-start.2
  195.8 2.5 copy-start.13
  306.8 18.8 %all-to-all-start.2 = ((bf16[2,4,32,2048]{3,2,0,1:T(8,128)(2,1)}), bf16[2,4,32,2048]{3,2,0,1:T(8,128)(2,1)}, u32[]{:S(2)}, u32[]{:S(2)}) async-start(bf16[2,4,32,2048]{3,2,0,1:T(8,128)(2,1)} %copy.60), calls=%async_computation.2 | async-start | bytes 2097152 | tf_op jit(solution)/shard_map/all_to_all | solution.py:221
  326.9 1.0 copy-start.11
